TPU v7x, 512 devices: a whole 4x4x16 slice. The times are simulated.
512 devices in a mesh: row: 16 (over z_lo, y), col: 32 (over x, z_hi, core).
Axes of the slice: x: 4, y: 4, z: 16 (z_hi: 4, z_lo: 4; z = z_hi * 4 + z_lo), core: 2. Of those that a mesh axis runs over, the one named last changes fastest.
Arguments:
- tiles: bfloat16 [16, 32, 32, 128, 128], P('row', 'col'), may hold values from -0.5 to 0.5
- tile_slots: int32 [16, 32, 32], P('row', 'col'), may hold values from 0 to 191, as said below
- tile_counts: int32 [16, 32], P('row', 'col'), may hold values from 8 to 32, as said below
- user_degree: int32 [32768], P('row'), may hold values from 1 to 64
- item_degree: int32 [49152], P('col'), may hold values from 1 to 64
- start_panel: float32 [64, 49152], P(None, ('col', 'row')), may hold values from -6 to 6
Outputs:
- left_panel: float32 [64, 32768], P(None, ('row', 'col'))
- right_panel: float32 [64, 49152], P(None, ('col', 'row'))
- left_factors: float32 [3, 64, 64], replicated
- right_factors: float32 [3, 64, 64], replicated
Inputs may be any that keep to these rules, and one draw needn't show every extreme that they name: `tile_slots`: within one grid cell the 32 slot numbers are distinct; slot s is local tile row s // 12 and local tile column s % 12; entries from position tile_counts on are padding. `tile_counts`: some grid cell holds 32 live tiles.
All inputs are finite; a program needn't handle non-finite values.
Results may differ from a plain program's by a relative error of at most 0.0005.
Values sent between devices are 32-bit elements; how exact they have to be, the bound alone decides.
No kernel may reach another device: no remote copies, remote signals or barrier semaphores. Data moves between devices by JAX's collectives and lax.ppermute only.
A program may use at most 64 MiB of HBM per device.

v0:
```python
import math
import jax
import jax.numpy as jnp
from jax import lax
from jax.sharding import PartitionSpec as P

STEPS = 3
HIGH = lax.Precision.HIGHEST


def gram_of(vectors):
    return jnp.einsum("bn,cn->bc", vectors, vectors, precision=HIGH)


def solve_lower(factor, vectors):
    return lax.linalg.triangular_solve(factor, vectors, left_side=True, lower=True)


def per_device(tiles, tile_slots, tile_counts, user_degree, item_degree, start_panel):
    tile_stack = tiles[0, 0].astype(jnp.float32)
    slot_list = tile_slots[0, 0]
    tile_total = tile_counts[0, 0]
    slot_count = tile_stack.shape[0]
    tile_width = tile_stack.shape[1]
    row_blocks = user_degree.shape[0] // tile_width
    col_blocks = item_degree.shape[0] // tile_width
    block_width = start_panel.shape[0]
    live_mask = jnp.arange(slot_count) < tile_total
    local_rows = slot_list // col_blocks
    local_cols = slot_list % col_blocks
    row_select = (
        (local_rows[:, None] == jnp.arange(row_blocks)[None, :]) & live_mask[:, None]
    ).astype(jnp.float32)
    col_select = (
        (local_cols[:, None] == jnp.arange(col_blocks)[None, :]) & live_mask[:, None]
    ).astype(jnp.float32)
    user_scale = lax.rsqrt(user_degree.astype(jnp.float32))
    item_scale = lax.rsqrt(item_degree.astype(jnp.float32))
    user_group = row_blocks * tile_width // lax.axis_size("col")
    item_group = col_blocks * tile_width // lax.axis_size("row")
    user_offset = lax.axis_index("col") * user_group
    item_offset = lax.axis_index("row") * item_group
    user_scale_own = lax.dynamic_slice_in_dim(user_scale, user_offset, user_group)
    item_scale_own = lax.dynamic_slice_in_dim(item_scale, item_offset, item_group)
    start_total = lax.psum(gram_of(start_panel), ("row", "col"))
    start_factor = jnp.linalg.cholesky(start_total)
    item_basis = solve_lower(start_factor, start_panel)
    user_basis = start_panel[:, :0]
    item_factor = start_factor
    user_list = []
    item_list = []
    for iteration in range(STEPS):
        scaled = item_basis * item_scale_own[None, :]
        item_full = lax.all_gather(scaled, "row", axis=1, tiled=True)
        forward_panel_blocks = item_full.reshape(block_width, col_blocks, tile_width)
        forward_chosen = jnp.take(forward_panel_blocks, local_cols, axis=1)
        forward_partial_value = jnp.einsum(
            "mrc,bmc->bmr", tile_stack, forward_chosen, precision=HIGH
        )
        forward_summed = jnp.einsum(
            "bmr,mk->bkr", forward_partial_value, row_select, precision=HIGH
        )
        forward = (
            lax.psum_scatter(
                forward_summed.reshape(block_width, row_blocks * tile_width),
                "col",
                scatter_dimension=1,
                tiled=True,
            )
            * user_scale_own[None, :]
        )
        if iteration > 0:
            forward = forward - jnp.dot(item_factor.T, user_basis, precision=HIGH)
        user_factor = jnp.linalg.cholesky(lax.psum(gram_of(forward), ("row", "col")))
        user_basis = solve_lower(user_factor, forward)
        scaled = user_basis * user_scale_own[None, :]
        user_full = lax.all_gather(scaled, "col", axis=1, tiled=True)
        panel_blocks = user_full.reshape(block_width, row_blocks, tile_width)
        chosen = jnp.take(panel_blocks, local_rows, axis=1)
        partial_value = jnp.einsum("mrc,bmr->bmc", tile_stack, chosen, precision=HIGH)
        summed = jnp.einsum("bmc,mk->bkc", partial_value, col_select, precision=HIGH)
        backward = (
            lax.psum_scatter(
                summed.reshape(block_width, col_blocks * tile_width),
                "row",
                scatter_dimension=1,
                tiled=True,
            )
            * item_scale_own[None, :]
        )
        backward = backward - jnp.dot(user_factor.T, item_basis, precision=HIGH)
        item_factor = jnp.linalg.cholesky(lax.psum(gram_of(backward), ("row", "col")))
        item_basis = solve_lower(item_factor, backward)
        user_list.append(user_factor)
        item_list.append(item_factor)
    user_total = row_blocks * tile_width * lax.axis_size("row")
    item_total = col_blocks * tile_width * lax.axis_size("col")
    return (
        math.sqrt(user_total) * user_basis,
        math.sqrt(item_total) * item_basis,
        jnp.stack(user_list),
        jnp.stack(item_list),
    )


def solution(mesh):
    in_specs = (
        P("row", "col", None, None, None),
        P("row", "col", None),
        P("row", "col"),
        P("row"),
        P("col"),
        P(None, ("col", "row")),
    )
    out_specs = (P(None, ("row", "col")), P(None, ("col", "row")), P(), P())
    return jax.shard_map(
        per_device, mesh=mesh, in_specs=in_specs, out_specs=out_specs, check_vma=False
    )
```

profile of v0, /device:TPU:1, one launch (start us, length us, event | category | flops | bytes accessed | tf_op | source)
XLA Modules:
  0.0 1727.9 jit_solution(9248479124465914468)
XLA Ops:
  9.7 111.2 %psum.49 = f32[64,64]{0,1:T(8,128)S(1)} all-reduce(f32[64,64]{0,1:T(8,128)S(1)} %fusion.153), channel_id=1, replica_groups=mesh['row'=16,'col'=32] {'row','col'}, use_global_device_ids=true, to_apply=%region_0.1 | all-reduce | flops 4096 | bytes 32768 | tf_op jit(solution)/shard_map/psum | solution.py:45
  120.9 5.8 cholesky.119
  128.1 4.9 custom-call.13
  134.1 33.8 %all-gather = f32[16,96,64]{1,2,0:T(8,128)S(1)} all-gather(f32[1,96,64]{1,2,0:T(8,128)S(1)} %multiply_bitcast_fusion.2), channel_id=1, replica_groups=mesh['row'=16,'col'=32] {'row'}, dimensions={0}, use_global_device_ids=true | all-gather | bytes 417792 | tf_op jit(solution)/shard_map/all_gather | solution.py:54
  174.6 110.4 %reduce-scatter.19.cloned.1.call-done = f32[64,64]{1,0:T(8,128)} async-done(((f32[2048,64]{1,0:T(8,128)}), f32[64,64]{1,0:T(8,128)}) %reduce-scatter.19.cloned.1.call-update) | async-done | bytes 16400
  286.0 101.8 %psum.50 = f32[64,64]{0,1:T(8,128)S(1)} all-reduce(f32[64,64]{0,1:T(8,128)S(1)} %fusion.81), channel_id=1, replica_groups=mesh['row'=16,'col'=32] {'row','col'}, use_global_device_ids=true, to_apply=%region_4.8 | all-reduce | flops 4096 | bytes 32768 | tf_op jit(solution)/shard_map/psum | solution.py:74
  388.0 5.8 cholesky.130
  395.1 4.9 custom-call.14
  400.4 57.0 %all_gather.19 = f32[64,2048]{0,1:T(8,128)S(1)} all-gather(f32[64,64]{0,1:T(8,128)S(1)} %copy.109), channel_id=1, replica_groups=mesh['row'=16,'col'=32] {'col'}, dimensions={1}, use_global_device_ids=true | all-gather | bytes 540672 | tf_op jit(solution)/shard_map/all_gather | solution.py:77
  461.6 71.2 %reduce-scatter.21.cloned.1.call-done = f32[96,64]{1,0:T(8,128)} async-done(((f32[1536,64]{1,0:T(8,128)}), f32[96,64]{1,0:T(8,128)}) %reduce-scatter.21.cloned.1.call-update) | async-done | bytes 24592
  534.8 112.8 %psum.51 = f32[64,64]{0,1:T(8,128)S(1)} all-reduce(f32[64,64]{0,1:T(8,128)S(1)} %fusion.154), channel_id=1, replica_groups=mesh['row'=16,'col'=32] {'row','col'}, use_global_device_ids=true, to_apply=%region_6.12 | all-reduce | flops 4096 | bytes 32768 | tf_op jit(solution)/shard_map/psum | solution.py:92
  647.7 5.8 cholesky.141
  654.9 4.9 custom-call.15
  660.0 36.4 %all-gather.1 = f32[16,96,64]{1,2,0:T(8,128)S(1)} all-gather(f32[1,96,64]{1,2,0:T(8,128)S(1)} %multiply_bitcast_fusion.1), channel_id=1, replica_groups=mesh['row'=16,'col'=32] {'row'}, dimensions={0}, use_global_device_ids=true | all-gather | bytes 417792 | tf_op jit(solution)/shard_map/all_gather | solution.py:54
  702.3 110.1 %reduce-scatter.23.cloned.1.call-done = f32[64,64]{1,0:T(8,128)} async-done(((f32[2048,64]{1,0:T(8,128)}), f32[64,64]{1,0:T(8,128)}) %reduce-scatter.23.cloned.1.call-update) | async-done | bytes 16400
  814.3 102.0 %psum.52 = f32[64,64]{0,1:T(8,128)S(1)} all-reduce(f32[64,64]{0,1:T(8,128)S(1)} %fusion.155), channel_id=1, replica_groups=mesh['row'=16,'col'=32] {'row','col'}, use_global_device_ids=true, to_apply=%region_8.14 | all-reduce | flops 4096 | bytes 32768 | tf_op jit(solution)/shard_map/psum | solution.py:74
  916.4 5.8 cholesky.152
  923.6 4.9 custom-call.16
  928.9 56.4 %all_gather.21 = f32[64,2048]{0,1:T(8,128)S(1)} all-gather(f32[64,64]{0,1:T(8,128)S(1)} %copy.120), channel_id=1, replica_groups=mesh['row'=16,'col'=32] {'col'}, dimensions={1}, use_global_device_ids=true | all-gather | bytes 540672 | tf_op jit(solution)/shard_map/all_gather | solution.py:77
  989.6 70.9 %reduce-scatter.25.cloned.1.call-done = f32[96,64]{1,0:T(8,128)} async-done(((f32[1536,64]{1,0:T(8,128)}), f32[96,64]{1,0:T(8,128)}) %reduce-scatter.25.cloned.1.call-update) | async-done | bytes 24592
  1062.5 113.1 %psum.53 = f32[64,64]{0,1:T(8,128)S(1)} all-reduce(f32[64,64]{0,1:T(8,128)S(1)} %fusion.156), channel_id=1, replica_groups=mesh['row'=16,'col'=32] {'row','col'}, use_global_device_ids=true, to_apply=%region_10.16 | all-reduce | flops 4096 | bytes 32768 | tf_op jit(solution)/shard_map/psum | solution.py:92
  1175.6 5.8 cholesky.163
  1182.8 4.9 custom-call.17
  1188.0 36.7 %all-gather.2 = f32[16,96,64]{1,2,0:T(8,128)S(1)} all-gather(f32[1,96,64]{1,2,0:T(8,128)S(1)} %multiply_bitcast_fusion), channel_id=1, replica_groups=mesh['row'=16,'col'=32] {'row'}, dimensions={0}, use_global_device_ids=true | all-gather | bytes 417792 | tf_op jit(solution)/shard_map/all_gather | solution.py:54
  1230.5 110.1 %reduce-scatter.27.cloned.1.call-done = f32[64,64]{1,0:T(8,128)} async-done(((f32[2048,64]{1,0:T(8,128)}), f32[64,64]{1,0:T(8,128)}) %reduce-scatter.27.cloned.1.call-update) | async-done | bytes 16400
  1342.5 101.8 %psum.54 = f32[64,64]{0,1:T(8,128)S(1)} all-reduce(f32[64,64]{0,1:T(8,128)S(1)} %fusion.157), channel_id=1, replica_groups=mesh['row'=16,'col'=32] {'row','col'}, use_global_device_ids=true, to_apply=%region_12.18 | all-reduce | flops 4096 | bytes 32768 | tf_op jit(solution)/shard_map/psum | solution.py:74
  1444.4 5.8 cholesky.174
  1451.6 4.9 custom-call.18
  1457.5 56.3 %all_gather.23 = f32[64,2048]{0,1:T(8,128)S(1)} all-gather(f32[64,64]{0,1:T(8,128)S(1)} %copy.131), channel_id=1, replica_groups=mesh['row'=16,'col'=32] {'col'}, dimensions={1}, use_global_device_ids=true | all-gather | bytes 540672 | tf_op jit(solution)/shard_map/all_gather | solution.py:77
  1518.7 73.4 %reduce-scatter.29.cloned.1.call-done = f32[96,64]{1,0:T(8,128)} async-done(((f32[1536,64]{1,0:T(8,128)}), f32[96,64]{1,0:T(8,128)}) %reduce-scatter.29.cloned.1.call-update) | async-done | bytes 24592
  1594.0 113.0 %psum.55 = f32[64,64]{0,1:T(8,128)S(1)} all-reduce(f32[64,64]{0,1:T(8,128)S(1)} %fusion.158), channel_id=1, replica_groups=mesh['row'=16,'col'=32] {'row','col'}, use_global_device_ids=true, to_apply=%region_14.20 | all-reduce | flops 4096 | bytes 32768 | tf_op jit(solution)/shard_map/psum | solution.py:92
  1707.1 5.8 cholesky.185
  (130 shorter events, 63.5 us)
Async XLA Ops:
  7.2 161.9 %copy-start = (bf16[1,1,32,128,128]{4,3,2,1,0:T(8,128)(2,1)S(1)}, bf16[1,1,32,128,128]{4,3,2,1,0:T(8,128)(2,1)}, u32[]{:S(2)}) copy-start(bf16[1,1,32,128,128]{4,3,2,1,0:T(8,128)(2,1)} %param.15) | copy-start | bytes 3145732
  7.2 277.8 %reduce-scatter.19.cloned.1.call-start = ((), (), s32[]{:S(2)}) async-start(), calls=%async_computation.6 | async-start | bytes 1081344
  8.0 0.7 copy-start.2
  127.5 5.6 copy-start.1
  173.7 359.1 %reduce-scatter.21.cloned.1.call-start = ((), (), s32[]{:S(2)}) async-start(), calls=%async_computation.7 | async-start | bytes 835584
  461.6 350.8 %reduce-scatter.23.cloned.1.call-start = ((), (), s32[]{:S(2)}) async-start(), calls=%async_computation.8 | async-start | bytes 1081344
  702.3 358.2 %reduce-scatter.25.cloned.1.call-start = ((), (), s32[]{:S(2)}) async-start(), calls=%async_computation.9 | async-start | bytes 835584
  989.5 351.1 %reduce-scatter.27.cloned.1.call-start = ((), (), s32[]{:S(2)}) async-start(), calls=%async_computation.10 | async-start | bytes 1081344
  1230.5 361.6 %reduce-scatter.29.cloned.1.call-start = ((), (), s32[]{:S(2)}) async-start(), calls=%async_computation.11 | async-start | bytes 835584
Sparse Core Ops, SparseCore 0:
  173.9 111.0 reduce-scatter.18
  461.7 71.0 reduce-scatter.20
  702.4 109.9 reduce-scatter.22
  989.6 70.8 reduce-scatter.24
  1230.6 109.9 reduce-scatter.26
  1518.1 73.8 reduce-scatter.28
where the time goes:
time: 1740 us; the launch traced here: 1730 us
  blocking collectives  1030 us (59%)
  waiting for transfers between devices  546 us (31%)
  other arithmetic  87.5 us (5%)
  matrix products  25.6 us (1%)
  local copies, waits for them, and re-layouts  20.4 us (1%)
    unnamed x12, waiting for transfers between devices  546 us
    psum x3, blocking collectives, per_device(): lax.psum(gram_of(backward), ('row', 'col'))  339 us
    psum x3, blocking collectives, per_device(): lax.psum(gram_of(forward), ('row', 'col'))  306 us
    all_gather x3, blocking collectives, per_device(): user_full = lax.all_gather(scaled, 'col', axis=1, tiled=True)  170 us
    psum x1, blocking collectives, per_device(): start_total = lax.psum(gram_of(start_panel), ('row', 'col'))  111 us
    all_gather x3, blocking collectives, per_device(): item_full = lax.all_gather(scaled, 'row', axis=1, tiled=True)  107 us
    another operation x8, other arithmetic, solve_lower(): lax.linalg.triangular_solve(factor, vectors, left_side=True, lower=True)  34.9 us
  transfers between devices with their start and end apart: 6, of which 6 were waited for; matrix products, arithmetic and copies ran while one was open for 0% of the time, Pallas kernels for 0%

commit v1 on v0

--- a/solution.py
+++ b/solution.py
@@ -42,7 +42,7 @@
     item_offset = lax.axis_index("row") * item_group
     user_scale_own = lax.dynamic_slice_in_dim(user_scale, user_offset, user_group)
     item_scale_own = lax.dynamic_slice_in_dim(item_scale, item_offset, item_group)
-    start_total = lax.psum(gram_of(start_panel), ("row", "col"))
+    start_total = lax.psum(lax.psum(gram_of(start_panel), "col"), "row")
     start_factor = jnp.linalg.cholesky(start_total)
     item_basis = solve_lower(start_factor, start_panel)
     user_basis = start_panel[:, :0]

time: 1740 us -> 1880 us (1.080)
  blocking collectives: 1030 us -> 1160 us
    psum x1 -> x2, blocking collectives: 111 us -> 237 us  [per_device(): start_total = lax.psum(lax.psum(gram_of(start_panel), 'col'), 'row')]
where the time goes in v1:
time: 1880 us; the launch traced here: 1870 us
  blocking collectives  1160 us (62%)
  waiting for transfers between devices  562 us (30%)
  other arithmetic  87.5 us (5%)
  matrix products  25.6 us (1%)
  local copies, waits for them, and re-layouts  20.4 us (1%)
    unnamed x12, waiting for transfers between devices  562 us
    psum x3, blocking collectives, per_device(): lax.psum(gram_of(backward), ('row', 'col'))  338 us
    psum x3, blocking collectives, per_device(): lax.psum(gram_of(forward), ('row', 'col'))  306 us
    psum x2, blocking collectives, per_device(): start_total = lax.psum(lax.psum(gram_of(start_panel), 'col'), 'row')  237 us
    all_gather x3, blocking collectives, per_device(): user_full = lax.all_gather(scaled, 'col', axis=1, tiled=True)  170 us
    all_gather x3, blocking collectives, per_device(): item_full = lax.all_gather(scaled, 'row', axis=1, tiled=True)  106 us
  transfers between devices with their start and end apart: 6, of which 6 were waited for; matrix products, arithmetic and copies ran while one was open for 0% of the time, Pallas kernels for 0%

profile of v1, /device:TPU:1, one launch (start us, length us, event | category | flops | bytes accessed | tf_op | source)
XLA Modules:
  0.0 1868.4 jit_solution(11363802105866357653)
XLA Ops:
  9.7 172.7 %psum.56 = f32[64,64]{0,1:T(8,128)S(1)} all-reduce(f32[64,64]{0,1:T(8,128)S(1)} %fusion.153), channel_id=1, replica_groups=mesh['row'=16,'col'=32] {'col'}, use_global_device_ids=true, to_apply=%region_0.1 | all-reduce | flops 4096 | bytes 32768 | tf_op jit(solution)/shard_map/psum | solution.py:45
  182.4 64.7 %psum.57 = f32[64,64]{0,1:T(8,128)S(1)} all-reduce(f32[64,64]{0,1:T(8,128)S(1)} %psum.56), channel_id=1, replica_groups=mesh['row'=16,'col'=32] {'row'}, use_global_device_ids=true, to_apply=%region_1.2 | all-reduce | flops 4096 | bytes 32768 | tf_op jit(solution)/shard_map/psum | solution.py:45
  247.2 5.8 cholesky.119
  254.4 4.9 custom-call.13
  260.3 32.5 %all-gather = f32[16,96,64]{1,2,0:T(8,128)S(1)} all-gather(f32[1,96,64]{1,2,0:T(8,128)S(1)} %multiply_bitcast_fusion.2), channel_id=1, replica_groups=mesh['row'=16,'col'=32] {'row'}, dimensions={0}, use_global_device_ids=true | all-gather | bytes 417792 | tf_op jit(solution)/shard_map/all_gather | solution.py:54
  299.6 126.7 %reduce-scatter.19.cloned.1.call-done = f32[64,64]{1,0:T(8,128)} async-done(((f32[2048,64]{1,0:T(8,128)}), f32[64,64]{1,0:T(8,128)}) %reduce-scatter.19.cloned.1.call-update) | async-done | bytes 16400
  427.3 101.9 %psum.58 = f32[64,64]{0,1:T(8,128)S(1)} all-reduce(f32[64,64]{0,1:T(8,128)S(1)} %fusion.81), channel_id=1, replica_groups=mesh['row'=16,'col'=32] {'row','col'}, use_global_device_ids=true, to_apply=%region_5.9 | all-reduce | flops 4096 | bytes 32768 | tf_op jit(solution)/shard_map/psum | solution.py:74
  529.2 5.8 cholesky.130
  536.4 4.9 custom-call.14
  541.7 56.8 %all_gather.19 = f32[64,2048]{0,1:T(8,128)S(1)} all-gather(f32[64,64]{0,1:T(8,128)S(1)} %copy.109), channel_id=1, replica_groups=mesh['row'=16,'col'=32] {'col'}, dimensions={1}, use_global_device_ids=true | all-gather | bytes 540672 | tf_op jit(solution)/shard_map/all_gather | solution.py:77
  602.7 72.3 %reduce-scatter.21.cloned.1.call-done = f32[96,64]{1,0:T(8,128)} async-done(((f32[1536,64]{1,0:T(8,128)}), f32[96,64]{1,0:T(8,128)}) %reduce-scatter.21.cloned.1.call-update) | async-done | bytes 24592
  677.0 112.7 %psum.59 = f32[64,64]{0,1:T(8,128)S(1)} all-reduce(f32[64,64]{0,1:T(8,128)S(1)} %fusion.154), channel_id=1, replica_groups=mesh['row'=16,'col'=32] {'row','col'}, use_global_device_ids=true, to_apply=%region_7.13 | all-reduce | flops 4096 | bytes 32768 | tf_op jit(solution)/shard_map/psum | solution.py:92
  789.8 5.8 cholesky.141
  797.0 4.9 custom-call.15
  802.2 36.3 %all-gather.1 = f32[16,96,64]{1,2,0:T(8,128)S(1)} all-gather(f32[1,96,64]{1,2,0:T(8,128)S(1)} %multiply_bitcast_fusion.1), channel_id=1, replica_groups=mesh['row'=16,'col'=32] {'row'}, dimensions={0}, use_global_device_ids=true | all-gather | bytes 417792 | tf_op jit(solution)/shard_map/all_gather | solution.py:54
  844.4 110.1 %reduce-scatter.23.cloned.1.call-done = f32[64,64]{1,0:T(8,128)} async-done(((f32[2048,64]{1,0:T(8,128)}), f32[64,64]{1,0:T(8,128)}) %reduce-scatter.23.cloned.1.call-update) | async-done | bytes 16400
  956.4 102.0 %psum.60 = f32[64,64]{0,1:T(8,128)S(1)} all-reduce(f32[64,64]{0,1:T(8,128)S(1)} %fusion.155), channel_id=1, replica_groups=mesh['row'=16,'col'=32] {'row','col'}, use_global_device_ids=true, to_apply=%region_9.15 | all-reduce | flops 4096 | bytes 32768 | tf_op jit(solution)/shard_map/psum | solution.py:74
  1058.5 5.8 cholesky.152
  1070.9 57.0 %all_gather.21 = f32[64,2048]{0,1:T(8,128)S(1)} all-gather(f32[64,64]{0,1:T(8,128)S(1)} %copy.120), channel_id=1, replica_groups=mesh['row'=16,'col'=32] {'col'}, dimensions={1}, use_global_device_ids=true | all-gather | bytes 540672 | tf_op jit(solution)/shard_map/all_gather | solution.py:77
  1132.2 70.9 %reduce-scatter.25.cloned.1.call-done = f32[96,64]{1,0:T(8,128)} async-done(((f32[1536,64]{1,0:T(8,128)}), f32[96,64]{1,0:T(8,128)}) %reduce-scatter.25.cloned.1.call-update) | async-done | bytes 24592
  1205.0 112.6 %psum.61 = f32[64,64]{0,1:T(8,128)S(1)} all-reduce(f32[64,64]{0,1:T(8,128)S(1)} %fusion.156), channel_id=1, replica_groups=mesh['row'=16,'col'=32] {'row','col'}, use_global_device_ids=true, to_apply=%region_11.17 | all-reduce | flops 4096 | bytes 32768 | tf_op jit(solution)/shard_map/psum | solution.py:92
  1317.8 5.8 cholesky.163
  1330.1 36.7 %all-gather.2 = f32[16,96,64]{1,2,0:T(8,128)S(1)} all-gather(f32[1,96,64]{1,2,0:T(8,128)S(1)} %multiply_bitcast_fusion), channel_id=1, replica_groups=mesh['row'=16,'col'=32] {'row'}, dimensions={0}, use_global_device_ids=true | all-gather | bytes 417792 | tf_op jit(solution)/shard_map/all_gather | solution.py:54
  1372.7 110.1 %reduce-scatter.27.cloned.1.call-done = f32[64,64]{1,0:T(8,128)} async-done(((f32[2048,64]{1,0:T(8,128)}), f32[64,64]{1,0:T(8,128)}) %reduce-scatter.27.cloned.1.call-update) | async-done | bytes 16400
  1484.7 101.8 %psum.62 = f32[64,64]{0,1:T(8,128)S(1)} all-reduce(f32[64,64]{0,1:T(8,128)S(1)} %fusion.157), channel_id=1, replica_groups=mesh['row'=16,'col'=32] {'row','col'}, use_global_device_ids=true, to_apply=%region_13.19 | all-reduce | flops 4096 | bytes 32768 | tf_op jit(solution)/shard_map/psum | solution.py:74
  1586.6 5.8 cholesky.174
  1593.8 4.9 custom-call.18
  1599.7 56.3 %all_gather.23 = f32[64,2048]{0,1:T(8,128)S(1)} all-gather(f32[64,64]{0,1:T(8,128)S(1)} %copy.131), channel_id=1, replica_groups=mesh['row'=16,'col'=32] {'col'}, dimensions={1}, use_global_device_ids=true | all-gather | bytes 540672 | tf_op jit(solution)/shard_map/all_gather | solution.py:77
  1660.9 71.7 %reduce-scatter.29.cloned.1.call-done = f32[96,64]{1,0:T(8,128)} async-done(((f32[1536,64]{1,0:T(8,128)}), f32[96,64]{1,0:T(8,128)}) %reduce-scatter.29.cloned.1.call-update) | async-done | bytes 24592
  1734.5 113.0 %psum.63 = f32[64,64]{0,1:T(8,128)S(1)} all-reduce(f32[64,64]{0,1:T(8,128)S(1)} %fusion.158), channel_id=1, replica_groups=mesh['row'=16,'col'=32] {'row','col'}, use_global_device_ids=true, to_apply=%region_15.21 | all-reduce | flops 4096 | bytes 32768 | tf_op jit(solution)/shard_map/psum | solution.py:92
  1847.7 5.8 cholesky.185
  1854.8 4.9 custom-call.19
  (131 shorter events, 68.4 us)
Async XLA Ops:
  7.2 286.9 %copy-start = (bf16[1,1,32,128,128]{4,3,2,1,0:T(8,128)(2,1)S(1)}, bf16[1,1,32,128,128]{4,3,2,1,0:T(8,128)(2,1)}, u32[]{:S(2)}) copy-start(bf16[1,1,32,128,128]{4,3,2,1,0:T(8,128)(2,1)} %param.15) | copy-start | bytes 3145732
  7.2 419.1 %reduce-scatter.19.cloned.1.call-start = ((), (), s32[]{:S(2)}) async-start(), calls=%async_computation.6 | async-start | bytes 1081344
  8.0 0.7 copy-start.2
  253.7 5.6 copy-start.1
  298.7 376.3 %reduce-scatter.21.cloned.1.call-start = ((), (), s32[]{:S(2)}) async-start(), calls=%async_computation.7 | async-start | bytes 835584
  602.7 351.8 %reduce-scatter.23.cloned.1.call-start = ((), (), s32[]{:S(2)}) async-start(), calls=%async_computation.8 | async-start | bytes 1081344
  844.3 358.7 %reduce-scatter.25.cloned.1.call-start = ((), (), s32[]{:S(2)}) async-start(), calls=%async_computation.9 | async-start | bytes 835584
  1132.1 350.7 %reduce-scatter.27.cloned.1.call-start = ((), (), s32[]{:S(2)}) async-start(), calls=%async_computation.10 | async-start | bytes 1081344
  1372.6 359.9 %reduce-scatter.29.cloned.1.call-start = ((), (), s32[]{:S(2)}) async-start(), calls=%async_computation.11 | async-start | bytes 835584
Sparse Core Ops, SparseCore 0:
  298.9 127.3 reduce-scatter.18
  602.8 72.1 reduce-scatter.20
  844.5 109.9 reduce-scatter.22
  1132.2 70.7 reduce-scatter.24
  1372.8 110.0 reduce-scatter.26
  1660.3 72.1 reduce-scatter.28
